TPU v7x, 32 devices: a whole 2x2x4 slice. The times are simulated.
32 devices in a mesh: group: 4 (over y, core), dom: 8 (over z, x).
Axes of the slice: x: 2, y: 2, z: 4, core: 2. Of those that a mesh axis runs over, the one named last changes fastest.
Arguments:
- features: float32 [4096, 1024], P(('group', 'dom')), may hold values from -6 to 6
- known_mask: int32 [4096], P(('group', 'dom')), may hold values 0 or 1
- local_tile: bfloat16 [4096, 128], P(('group', 'dom')), may hold values from 0 to 1.5, as said below
- peer_tile: bfloat16 [4096, 256], P(('group', 'dom')), may hold values from 0 to 1.5, as said below
- cross_tile: bfloat16 [4096, 128], P(('group', 'dom')), may hold values from 0 to 1.5, as said below
- peer_rows: int32 [4, 8, 8, 32], P('group', 'dom'), may hold values from 0 to 127
- cross_rows: int32 [4, 8, 4, 32], P('group', 'dom'), may hold values from 0 to 127
- labels: int32 [4096], P(('group', 'dom')), may hold values from 0 to 18
- first_weight: bfloat16 [1024, 1024], replicated, may hold values from -0.1875 to 0.1875
- first_bias: float32 [1024], replicated, may hold values from -3 to 3
- second_weight: bfloat16 [1024, 19], replicated, may hold values from -60 to 60
- second_bias: float32 [19], replicated, may hold values from -3 to 3
Outputs:
- imputed: float32 [4096, 1024], P(('group', 'dom'))
- grad_first: float32 [1024, 1024], P('dom')
- grad_first_bias: float32 [1024], replicated
- grad_second: float32 [1024, 19], replicated
- grad_second_bias: float32 [19], replicated
Inputs may be any that keep to these rules, and one draw needn't show every extreme that they name: `local_tile`: each entry is 0 or lies in 0.5 to 1.5; a fraction of about 8 / 128 is nonzero. `peer_tile`: each entry is 0 or lies in 0.5 to 1.5; a fraction of about 6 / 256 is nonzero. `cross_tile`: each entry is 0 or lies in 0.5 to 1.5; a fraction of about 4 / 128 is nonzero.
All inputs are finite; a program needn't handle non-finite values. No bound on the sum of `known_mask` on one device may be relied on, other than what follows from the above.
Results may differ from a plain program's by a relative error of at most 0.0041.
Values sent between devices are 32-bit elements; how exact they have to be, the bound alone decides.
A program may use at most 64 MiB of HBM per device.

v0:
```python
import math

import jax
import jax.numpy as jnp
from jax import lax
from jax.sharding import PartitionSpec as P

SWEEPS = 3


def fetch_halos(current, peer_list, cross_list):
    width = current.shape[1]
    outgoing = current[peer_list.reshape(-1)].reshape(peer_list.shape[2], peer_list.shape[3], width)
    incoming = lax.all_to_all(outgoing, "dom", split_axis=0, concat_axis=0, tiled=True)
    leaving = current[cross_list.reshape(-1)].reshape(
        cross_list.shape[2], cross_list.shape[3], width
    )
    arriving = lax.all_to_all(leaving, "group", split_axis=0, concat_axis=0, tiled=True)
    return (incoming.reshape(-1, width), arriving.reshape(-1, width))


def local(
    features,
    known_mask,
    local_tile,
    peer_tile,
    cross_tile,
    peer_rows,
    cross_rows,
    labels,
    first_weight,
    first_bias,
    second_weight,
    second_bias,
):
    highest = lax.Precision.HIGHEST
    keep = (known_mask == 1)[:, None]
    current = jnp.where(keep, features, jnp.float32(0.0))
    local_full = local_tile.astype(jnp.float32)
    peer_full = peer_tile.astype(jnp.float32)
    cross_full = cross_tile.astype(jnp.float32)
    degree = (
        1.0 + jnp.sum(local_full, axis=1) + jnp.sum(peer_full, axis=1) + jnp.sum(cross_full, axis=1)
    )
    degree = degree[:, None]
    for sweep in range(SWEEPS):
        incoming, arriving = fetch_halos(current, peer_rows, cross_rows)
        summed = current + jnp.dot(
            local_full, current, precision=highest, preferred_element_type=jnp.float32
        )
        summed = summed + jnp.dot(
            peer_full, incoming, precision=highest, preferred_element_type=jnp.float32
        )
        summed = summed + jnp.dot(
            cross_full, arriving, precision=highest, preferred_element_type=jnp.float32
        )
        current = jnp.where(keep, features, summed / degree)
    inputs = current.astype(jnp.bfloat16)
    pre = jnp.dot(inputs, first_weight, preferred_element_type=jnp.float32) + first_bias
    sigma = jax.nn.sigmoid(pre)
    active = (pre * sigma).astype(jnp.bfloat16)
    logits = jnp.dot(active, second_weight, preferred_element_type=jnp.float32) + second_bias
    shifted = logits - jnp.max(logits, axis=1, keepdims=True)
    expo = jnp.exp(shifted)
    probs = expo / jnp.sum(expo, axis=1, keepdims=True)
    classes = second_weight.shape[1]
    onehot = (labels[:, None] == jnp.arange(classes, dtype=jnp.int32)[None, :]).astype(jnp.float32)
    total_nodes = features.shape[0] * lax.axis_size("group") * lax.axis_size("dom")
    dlogits = (probs - onehot) / jnp.float32(math.sqrt(total_nodes))
    dlogits_b = dlogits.astype(jnp.bfloat16)
    second_bias_term = jnp.sum(dlogits, axis=0)
    second_term = lax.dot_general(
        active, dlogits_b, (((0,), (0,)), ((), ())), preferred_element_type=jnp.float32
    )
    back = lax.dot_general(
        dlogits_b, second_weight, (((1,), (1,)), ((), ())), preferred_element_type=jnp.float32
    )
    dpre = (back * sigma * (1.0 + pre * (1.0 - sigma))).astype(jnp.bfloat16)
    first_bias_term = jnp.sum(dpre.astype(jnp.float32), axis=0)
    share = lax.psum_scatter(
        lax.dot_general(inputs, dpre, (((0,), (0,)), ((), ())), preferred_element_type=jnp.float32),
        "dom",
        scatter_dimension=0,
        tiled=True,
    )
    grad_first = lax.psum(share, "group")
    grad_first_bias, grad_second, grad_second_bias = lax.psum(
        (first_bias_term, second_term, second_bias_term), ("group", "dom")
    )
    return (current, grad_first, grad_first_bias, grad_second, grad_second_bias)


def solution(mesh):
    in_specs = (
        P(("group", "dom"), None),
        P(("group", "dom")),
        P(("group", "dom"), None),
        P(("group", "dom"), None),
        P(("group", "dom"), None),
        P("group", "dom", None, None),
        P("group", "dom", None, None),
        P(("group", "dom")),
        P(),
        P(),
        P(),
        P(),
    )
    out_specs = (P(("group", "dom"), None), P("dom", None), P(), P(), P())
    return jax.shard_map(local, mesh=mesh, in_specs=in_specs, out_specs=out_specs, check_vma=False)
```

profile of v0, /device:TPU:1, one launch (start us, length us, event | category | flops | bytes accessed | tf_op | source)
XLA Modules:
  0.0 361.4 jit_solution(1645723564046518858)
XLA Ops:
  13.9 4.3 %all-to-all-start.1 = ((f32[4,32,1024]{2,1,0:T(8,128)}), f32[4,32,1024]{2,1,0:T(8,128)}, u32[]{:S(2)}, u32[]{:S(2)}) async-start(f32[4,32,1024]{2,1,0:T(8,128)} %bitcast.91), calls=%async_computation.1 | async-start | bytes 1048576 | tf_op jit(solution)/shard_map/all_to_all | solution.py:18
  18.2 2.1 gather_fusion
  20.3 6.0 %all-to-all-done.1 = f32[4,32,1024]{2,1,0:T(8,128)} async-done(((f32[4,32,1024]{2,1,0:T(8,128)}), f32[4,32,1024]{2,1,0:T(8,128)}, u32[]{:S(2)}, u32[]{:S(2)}) %all-to-all-start.1) | async-done | bytes 524320 | tf_op jit(solution)/shard_map/all_to_all | solution.py:18
  26.3 6.6 %all-to-all-start = ((f32[8,32,1024]{2,1,0:T(8,128)}), f32[8,32,1024]{2,1,0:T(8,128)}, u32[]{:S(2)}, u32[]{:S(2)}) async-start(f32[8,32,1024]{2,1,0:T(8,128)} %bitcast.88), calls=%async_computation | async-start | bytes 2097152 | tf_op jit(solution)/shard_map/all_to_all | solution.py:14
  34.8 22.8 %all-to-all-done = f32[8,32,1024]{2,1,0:T(8,128)} async-done(((f32[8,32,1024]{2,1,0:T(8,128)}), f32[8,32,1024]{2,1,0:T(8,128)}, u32[]{:S(2)}, u32[]{:S(2)}) %all-to-all-start) | async-done | bytes 1048608 | tf_op jit(solution)/shard_map/all_to_all | solution.py:14
  57.6 2.2 convolution_bitcast_fusion.8
  63.9 6.3 %all-to-all-start.3 = ((f32[4,32,1024]{2,1,0:T(8,128)}), f32[4,32,1024]{2,1,0:T(8,128)}, u32[]{:S(2)}, u32[]{:S(2)}) async-start(f32[4,32,1024]{2,1,0:T(8,128)} %bitcast.93), calls=%async_computation.3 | async-start | bytes 1048576 | tf_op jit(solution)/shard_map/all_to_all | solution.py:18
  72.3 5.9 %all-to-all-done.3 = f32[4,32,1024]{2,1,0:T(8,128)} async-done(((f32[4,32,1024]{2,1,0:T(8,128)}), f32[4,32,1024]{2,1,0:T(8,128)}, u32[]{:S(2)}, u32[]{:S(2)}) %all-to-all-start.3) | async-done | bytes 524320 | tf_op jit(solution)/shard_map/all_to_all | solution.py:18
  78.2 4.4 %all-to-all-start.2 = ((f32[8,32,1024]{2,1,0:T(8,128)}), f32[8,32,1024]{2,1,0:T(8,128)}, u32[]{:S(2)}, u32[]{:S(2)}) async-start(f32[8,32,1024]{2,1,0:T(8,128)} %bitcast.90), calls=%async_computation.2 | async-start | bytes 2097152 | tf_op jit(solution)/shard_map/all_to_all | solution.py:14
  82.6 2.4 convolution_bitcast_fusion.2
  85.0 22.5 %all-to-all-done.2 = f32[8,32,1024]{2,1,0:T(8,128)} async-done(((f32[8,32,1024]{2,1,0:T(8,128)}), f32[8,32,1024]{2,1,0:T(8,128)}, u32[]{:S(2)}, u32[]{:S(2)}) %all-to-all-start.2) | async-done | bytes 1048608 | tf_op jit(solution)/shard_map/all_to_all | solution.py:14
  107.5 2.2 convolution_bitcast_fusion.7
  109.8 2.2 fusion.11
  114.8 5.9 %all-to-all-start.5 = ((f32[4,32,1024]{2,1,0:T(8,128)}), f32[4,32,1024]{2,1,0:T(8,128)}, u32[]{:S(2)}, u32[]{:S(2)}) async-start(f32[4,32,1024]{2,1,0:T(8,128)} %bitcast.92), calls=%async_computation.5 | async-start | bytes 1048576 | tf_op jit(solution)/shard_map/all_to_all | solution.py:18
  122.8 5.9 %all-to-all-done.5 = f32[4,32,1024]{2,1,0:T(8,128)} async-done(((f32[4,32,1024]{2,1,0:T(8,128)}), f32[4,32,1024]{2,1,0:T(8,128)}, u32[]{:S(2)}, u32[]{:S(2)}) %all-to-all-start.5) | async-done | bytes 524320 | tf_op jit(solution)/shard_map/all_to_all | solution.py:18
  128.7 4.2 %all-to-all-start.4 = ((f32[8,32,1024]{2,1,0:T(8,128)}), f32[8,32,1024]{2,1,0:T(8,128)}, u32[]{:S(2)}, u32[]{:S(2)}) async-start(f32[8,32,1024]{2,1,0:T(8,128)} %bitcast.89), calls=%async_computation.4 | async-start | bytes 2097152 | tf_op jit(solution)/shard_map/all_to_all | solution.py:14
  133.0 2.4 convolution_bitcast_fusion
  135.4 22.5 %all-to-all-done.4 = f32[8,32,1024]{2,1,0:T(8,128)} async-done(((f32[8,32,1024]{2,1,0:T(8,128)}), f32[8,32,1024]{2,1,0:T(8,128)}, u32[]{:S(2)}, u32[]{:S(2)}) %all-to-all-start.4) | async-done | bytes 1048608 | tf_op jit(solution)/shard_map/all_to_all | solution.py:14
  157.9 2.2 convolution_bitcast_fusion.6
  163.4 2.6 fusion.17
  167.0 87.1 %reduce-scatter.2.cloned.1.call-done = f32[128,1024]{1,0:T(8,128)} async-done(((f32[1024,1024]{1,0:T(8,128)}), f32[128,1024]{1,0:T(8,128)}) %reduce-scatter.2.cloned.1.call-update) | async-done | bytes 524304 | tf_op jit(solution)/shard_map/reduce_scatter | solution.py:80
  255.3 40.4 %all-reduce = (f32[1024]{0:T(1024)}, f32[19]{0:T(128)}) all-reduce(f32[1024]{0:T(1024)S(1)} %get-tuple-element.16, f32[19]{0:T(128)S(1)} %fusion.26), channel_id=1, replica_groups=mesh['group'=4,'dom'=8] {'group','dom'}, use_global_device_ids=true, to_apply=%region_8.9 | all-reduce | flops 1043 | bytes 8344 | tf_op jit(solution)/shard_map/psum | solution.py:87
  295.6 19.9 %all-reduce.6.cloned.1.call-done = f32[1024,19]{0,1:T(8,128)} async-done(((f32[1024,19]{0,1:T(8,128)}), f32[1024,19]{0,1:T(8,128)}) %all-reduce.6.cloned.1.call-update) | async-done | bytes 77840 | tf_op jit(solution)/shard_map/psum | solution.py:87
  315.5 35.1 %all-reduce.4.cloned.1.call-done = f32[128,1024]{1,0:T(8,128)} async-done(((f32[128,1024]{1,0:T(8,128)}), f32[128,1024]{1,0:T(8,128)}) %all-reduce.4.cloned.1.call-update) | async-done | bytes 524304 | tf_op jit(solution)/shard_map/psum | solution.py:86
  (60 shorter events, 27.5 us)
Async XLA Ops:
  8.0 154.0 %copy-start = (bf16[1024,1024]{1,0:T(8,128)(2,1)S(1)}, bf16[1024,1024]{1,0:T(8,128)(2,1)}, u32[]{:S(2)}) copy-start(bf16[1024,1024]{1,0:T(8,128)(2,1)} %param.20) | copy-start | bytes 6291460
  8.0 4.1 %copy-start.7 = (s32[1,1,4,32]{3,2,1,0:T(4,128)S(1)}, s32[1,1,4,32]{3,2,1,0:T(4,128)}, u32[]{:S(2)}) copy-start(s32[1,1,4,32]{3,2,1,0:T(4,128)} %param.18) | copy-start | bytes 1540
  12.3 5.9 %copy-start.5 = (s32[1,1,8,32]{3,2,1,0:T(8,128)S(1)}, s32[1,1,8,32]{3,2,1,0:T(8,128)}, u32[]{:S(2)}) copy-start(s32[1,1,8,32]{3,2,1,0:T(8,128)} %param.17) | copy-start | bytes 3076
  13.9 12.5 %all-to-all-start.1 = ((f32[4,32,1024]{2,1,0:T(8,128)}), f32[4,32,1024]{2,1,0:T(8,128)}, u32[]{:S(2)}, u32[]{:S(2)}) async-start(f32[4,32,1024]{2,1,0:T(8,128)} %bitcast.91), calls=%async_computation.1 | async-start | bytes 1048576 | tf_op jit(solution)/shard_map/all_to_all | solution.py:18
  20.3 12.6 %copy-start.2 = (bf16[128,256]{1,0:T(8,128)(2,1)S(1)}, bf16[128,256]{1,0:T(8,128)(2,1)}, u32[]{:S(2)}) copy-start(bf16[128,256]{1,0:T(8,128)(2,1)} %param.15) | copy-start | bytes 196612
  20.3 12.8 %copy-start.3 = (bf16[128,128]{1,0:T(8,128)(2,1)S(1)}, bf16[128,128]{1,0:T(8,128)(2,1)}, u32[]{:S(2)}) copy-start(bf16[128,128]{1,0:T(8,128)(2,1)} %param.16) | copy-start | bytes 98308
  20.3 12.8 %copy-start.4 = (bf16[128,128]{1,0:T(8,128)(2,1)S(1)}, bf16[128,128]{1,0:T(8,128)(2,1)}, u32[]{:S(2)}) copy-start(bf16[128,128]{1,0:T(8,128)(2,1)} %param.14) | copy-start | bytes 98308
  26.3 31.3 %all-to-all-start = ((f32[8,32,1024]{2,1,0:T(8,128)}), f32[8,32,1024]{2,1,0:T(8,128)}, u32[]{:S(2)}, u32[]{:S(2)}) async-start(f32[8,32,1024]{2,1,0:T(8,128)} %bitcast.88), calls=%async_computation | async-start | bytes 2097152 | tf_op jit(solution)/shard_map/all_to_all | solution.py:14
  63.9 14.3 %all-to-all-start.3 = ((f32[4,32,1024]{2,1,0:T(8,128)}), f32[4,32,1024]{2,1,0:T(8,128)}, u32[]{:S(2)}, u32[]{:S(2)}) async-start(f32[4,32,1024]{2,1,0:T(8,128)} %bitcast.93), calls=%async_computation.3 | async-start | bytes 1048576 | tf_op jit(solution)/shard_map/all_to_all | solution.py:18
  78.2 31.6 %copy-start.1 = (f32[128,1024]{0,1:T(8,128)S(1)}, f32[128,1024]{0,1:T(8,128)}, u32[]{:S(2)}) copy-start(f32[128,1024]{0,1:T(8,128)} %fusion.7) | copy-start | bytes 1572868
  78.2 29.3 %all-to-all-start.2 = ((f32[8,32,1024]{2,1,0:T(8,128)}), f32[8,32,1024]{2,1,0:T(8,128)}, u32[]{:S(2)}, u32[]{:S(2)}) async-start(f32[8,32,1024]{2,1,0:T(8,128)} %bitcast.90), calls=%async_computation.2 | async-start | bytes 2097152 | tf_op jit(solution)/shard_map/all_to_all | solution.py:14
  114.8 13.8 %all-to-all-start.5 = ((f32[4,32,1024]{2,1,0:T(8,128)}), f32[4,32,1024]{2,1,0:T(8,128)}, u32[]{:S(2)}, u32[]{:S(2)}) async-start(f32[4,32,1024]{2,1,0:T(8,128)} %bitcast.92), calls=%async_computation.5 | async-start | bytes 1048576 | tf_op jit(solution)/shard_map/all_to_all | solution.py:18
  128.7 29.2 %all-to-all-start.4 = ((f32[8,32,1024]{2,1,0:T(8,128)}), f32[8,32,1024]{2,1,0:T(8,128)}, u32[]{:S(2)}, u32[]{:S(2)}) async-start(f32[8,32,1024]{2,1,0:T(8,128)} %bitcast.89), calls=%async_computation.4 | async-start | bytes 2097152 | tf_op jit(solution)/shard_map/all_to_all | solution.py:14
  132.9 121.2 %reduce-scatter.2.cloned.1.call-start = ((), (), s32[]{:S(2)}) async-start(), calls=%async_computation.7 | async-start | bytes 4718592 | tf_op jit(solution)/shard_map/reduce_scatter | solution.py:80
  157.9 4.1 %copy-start.9 = (f32[1024]{0:T(1024)S(1)}, f32[1024]{0:T(1024)}, u32[]{:S(2)}) copy-start(f32[1024]{0:T(1024)} %param.21) | copy-start | bytes 12292
  162.0 0.8 copy-start.8
  162.0 0.8 copy-start.10
  162.0 1.0 copy-start.6
  166.1 149.4 %all-reduce.6.cloned.1.call-start = ((), (), s32[]{:S(2)}) async-start(), calls=%async_computation.9 | async-start | bytes 196608 | tf_op jit(solution)/shard_map/psum | solution.py:87
  166.9 183.6 %all-reduce.4.cloned.1.call-start = ((), (), s32[]{:S(2)}) async-start(), calls=%async_computation.8 | async-start | bytes 1048576 | tf_op jit(solution)/shard_map/psum | solution.py:86
Sparse Core Ops, SparseCore 0:
  166.2 87.8 reduce-scatter.1
Sparse Core Ops, SparseCore 1:
  172.7 142.7 all-reduce.5
  317.7 32.8 all-reduce.3
where the time goes:
time: 365 us; the launch traced here: 361 us
  waiting for transfers between devices  228 us (62%)
  blocking collectives  40.4 us (11%)
  starting transfers between devices  31.9 us (9%)
  matrix products  23 us (6%)
  local copies, waits for them, and re-layouts  20.8 us (6%)
  between operations  15.7 us (4%)
    reduce_scatter x1, waiting for transfers between devices, local(): lax.psum_scatter(lax.dot_general(inputs, dpre, (((0,), (0,)), ((), ())),...  87.1 us
    all_to_all x3, waiting for transfers between devices, fetch_halos(): lax.all_to_all(outgoing, 'dom', split_axis=0, concat_axis=0, tiled=True)  67.8 us
    psum x1, blocking collectives, local(): lax.psum((first_bias_term, second_term, second_bias_term), ('group', 'dom'))  40.4 us
    psum x1, waiting for transfers between devices, local(): grad_first = lax.psum(share, 'group')  35.1 us
    psum x1, waiting for transfers between devices, local(): lax.psum((first_bias_term, second_term, second_bias_term), ('group', 'dom'))  19.9 us
    all_to_all x3, waiting for transfers between devices, fetch_halos(): lax.all_to_all(leaving, 'group', split_axis=0, concat_axis=0, tiled=True)  17.8 us
    all_to_all x3, starting transfers between devices, fetch_halos(): lax.all_to_all(leaving, 'group', split_axis=0, concat_axis=0, tiled=True)  16.5 us
    all_to_all x3, starting transfers between devices, fetch_halos(): lax.all_to_all(outgoing, 'dom', split_axis=0, concat_axis=0, tiled=True)  15.2 us
  transfers between devices with their start and end apart: 9, of which 9 were waited for; matrix products, arithmetic and copies ran while one was open for 4% of the time, Pallas kernels for 0%

commit v1 on v0

v1 whole, which is shorter than its diff:
```python
import functools
import math

import jax
import jax.numpy as jnp
from jax import lax
from jax.experimental import pallas as pl
from jax.experimental.pallas import tpu as pltpu
from jax.sharding import PartitionSpec as P

SWEEPS = 3
CHUNKS = 2
MESH = pl.DeviceIdType.MESH


def split(x):
    high = x.astype(jnp.bfloat16)
    low = (x - high.astype(jnp.float32)).astype(jnp.bfloat16)
    return high, low


def two_pass(a, parts):
    out = jnp.dot(a, parts[0], preferred_element_type=jnp.float32)
    return out + jnp.dot(a, parts[1], preferred_element_type=jnp.float32)


def bits_of(name, n):
    return [(name, b) for b in range(n.bit_length() - 1)]


def reduce_orders(n_group, n_dom):
    group, dom = bits_of("group", n_group), bits_of("dom", n_dom)
    bulk_a = group + dom
    bulk_b = group[:1] + dom[:1] + group[1:] + dom[1:]
    small = dom[1:] + group[:1] + dom[:1] + group[1:]
    return [bulk_a, bulk_b], small


def kernel(
    n_group, n_dom, peer_slots, cross_slots, total_nodes,
    feat_ref, keep_ref, local_ref, peer_ref, cross_ref, pick_ref, label_ref,
    w1_hbm, b1_ref, w2_ref, b2_ref,
    imputed_ref, grad_ref, small_ref,
    w1_ref, cur, send, recv, inputs, grads, incoming, small_acc, small_in, gathered,
    w1_sem, send_sem, recv_sem, bulk_send, bulk_recv, small_send, small_recv,
    out_send, out_recv,
):
    sizes = {"group": n_group, "dom": n_dom}
    me = {name: lax.axis_index(name) for name in sizes}
    rows, width = feat_ref.shape
    cols = width // CHUNKS
    peer_total = n_dom * peer_slots

    load_w1 = pltpu.make_async_copy(w1_hbm, w1_ref, w1_sem)
    load_w1.start()
    barrier = pltpu.get_barrier_semaphore()
    for name, n in sizes.items():
        for k in range(1, n):
            pl.semaphore_signal(
                barrier, inc=1, device_id={name: lax.rem(me[name] + k, n)}, device_id_type=MESH
            )

    local = local_ref[...]
    halo = jnp.concatenate([peer_ref[...], cross_ref[...]], axis=1)
    degree = (
        1.0
        + jnp.sum(local.astype(jnp.float32), axis=1, keepdims=True)
        + jnp.sum(halo.astype(jnp.float32), axis=1, keepdims=True)
    )
    keep = keep_ref[...] == 1
    pick = pick_ref[...]

    def exchange(sweep, c, parts):
        out = send.at[sweep, c]
        into = recv.at[sweep, c]
        send[sweep, c] = two_pass(pick, parts)
        for name, base, slots in (("dom", 0, peer_slots), ("group", peer_total, cross_slots)):
            n = sizes[name]
            mine = pl.ds(pl.multiple_of(base + me[name] * slots, slots), slots)
            for k in list(range(1, n)):
                there = lax.rem(me[name] + k, n)
                pltpu.make_async_remote_copy(
                    src_ref=out.at[pl.ds(pl.multiple_of(base + there * slots, slots), slots)],
                    dst_ref=into.at[mine],
                    send_sem=send_sem.at[sweep, c],
                    recv_sem=recv_sem.at[sweep, c],
                    device_id={name: there},
                    device_id_type=MESH,
                ).start()
            pltpu.make_async_copy(out.at[mine], into.at[mine], recv_sem.at[sweep, c]).start()

    for c in range(CHUNKS):
        now = jnp.where(keep, feat_ref[:, c * cols:(c + 1) * cols], jnp.float32(0.0))
        cur[c] = now
        if c == 0:
            pl.semaphore_wait(barrier, n_dom - 1 + n_group - 1)
        exchange(0, c, split(now))
    for sweep in range(SWEEPS):
        for c in range(CHUNKS):
            area = slice(c * cols, (c + 1) * cols)
            now = cur[c]
            summed = now + two_pass(local, split(now))
            pltpu.make_async_copy(
                recv.at[sweep, c], recv.at[sweep, c], recv_sem.at[sweep, c]
            ).wait()
            summed = summed + two_pass(halo, split(recv[sweep, c]))
            now = jnp.where(keep, feat_ref[:, area], summed / degree)
            if sweep + 1 < SWEEPS:
                cur[c] = now
                exchange(sweep + 1, c, split(now))
            else:
                imputed_ref[:, area] = now
                inputs[:, area] = now.astype(jnp.bfloat16)

    load_w1.wait()
    pre = jnp.dot(inputs[...], w1_ref[...], preferred_element_type=jnp.float32) + b1_ref[...]
    sigma = jax.nn.sigmoid(pre)
    active = (pre * sigma).astype(jnp.bfloat16)
    w2 = w2_ref[...]
    logits = jnp.dot(active, w2, preferred_element_type=jnp.float32) + b2_ref[...]
    shifted = logits - jnp.max(logits, axis=1, keepdims=True)
    expo = jnp.exp(shifted)
    probs = expo / jnp.sum(expo, axis=1, keepdims=True)
    classes = w2.shape[1]
    hot = label_ref[...] == lax.broadcasted_iota(jnp.int32, (rows, classes), 1)
    dlogits = (probs - hot.astype(jnp.float32)) / jnp.float32(math.sqrt(total_nodes))
    dlogits_b = dlogits.astype(jnp.bfloat16)
    back = lax.dot_general(
        dlogits_b, w2, (((1,), (1,)), ((), ())), preferred_element_type=jnp.float32
    )
    dpre32 = back * sigma * (1.0 + pre * (1.0 - sigma))
    dpre = dpre32.astype(jnp.bfloat16)

    orders, small_order = reduce_orders(n_group, n_dom)
    stages = len(small_order)

    def bit(name, b):
        return lax.rem(lax.div(me[name], 1 << b), 2)

    def partner(name, b):
        return {name: me[name] + (1 << b) * (1 - 2 * bit(name, b))}

    small_acc[0] = jnp.zeros(small_acc.shape[1:], jnp.float32)
    small_acc[0, :classes] = lax.dot_general(
        dlogits_b, active, (((0,), (0,)), ((), ())), preferred_element_type=jnp.float32
    )
    small_acc[0, classes:classes + 1] = jnp.sum(dpre.astype(jnp.float32), axis=0, keepdims=True)
    small_acc[0, classes + 1:classes + 2, :classes] = jnp.sum(dlogits, axis=0, keepdims=True)

    def small_copy(s):
        return pltpu.make_async_remote_copy(
            src_ref=small_acc.at[s],
            dst_ref=small_in.at[s],
            send_sem=small_send.at[s],
            recv_sem=small_recv.at[s],
            device_id=partner(*small_order[s]),
            device_id_type=MESH,
        )

    deep, share = width // n_dom, width // n_dom // n_group
    blocks = n_group * n_dom

    def place(order, where):
        at = 0
        for name, b in order:
            at = 2 * at + ((where[name] >> b) & 1)
        return at

    start, length, offset = [0] * CHUNKS, blocks, 0
    copies = [[] for _ in range(CHUNKS)]

    def bulk_start(s, h):
        half = blocks >> (s + 1)
        name, b = orders[h][s]
        mine = bit(name, b)
        copy = pltpu.make_async_remote_copy(
            src_ref=grads.at[h, pl.ds(start[h] + (1 - mine) * half, half)],
            dst_ref=incoming.at[h, pl.ds(blocks - 2 * half, half)],
            send_sem=bulk_send.at[h, s],
            recv_sem=bulk_recv.at[h, s],
            device_id=partner(name, b),
            device_id_type=MESH,
        )
        copy.start()
        copies[h].append(copy)
        start[h] = start[h] + mine * half

    small_copies = [small_copy(0)]
    small_copies[0].start()
    for h in range(CHUNKS):
        units = dpre.shape[1] // CHUNKS
        part = dpre[:, h * units:(h + 1) * units]
        for d in range(n_dom):
            term = lax.dot_general(
                inputs[:, d * deep:(d + 1) * deep], part, (((0,), (0,)), ((), ())),
                preferred_element_type=jnp.float32,
            )
            for g in range(n_group):
                grads[h, place(orders[h], {"group": g, "dom": d})] = term[g * share:(g + 1) * share]
        bulk_start(0, h)
    for s in range(stages):
        half = blocks >> (s + 1)
        for h in range(CHUNKS):
            copies[h][s].wait_recv()
            kept = pl.ds(start[h], half)
            grads[h, kept] = grads[h, kept] + incoming[h, pl.ds(blocks - 2 * half, half)]
            if s + 1 < stages:
                bulk_start(s + 1, h)
        small_copies[s].wait_recv()
        small_acc[s + 1] = small_acc[s] + small_in[s]
        if s + 1 < stages:
            small_copies.append(small_copy(s + 1))
            small_copies[-1].start()

    g_me = me["group"]
    for h in range(CHUNKS):
        for k in range(1, n_group):
            pltpu.make_async_remote_copy(
                src_ref=grads.at[h, start[h]],
                dst_ref=gathered.at[h, g_me],
                send_sem=out_send.at[h],
                recv_sem=out_recv.at[h],
                device_id={"group": lax.rem(g_me + k, n_group)},
                device_id_type=MESH,
            ).start()
        pltpu.make_async_copy(
            grads.at[h, start[h]], gathered.at[h, g_me], out_recv.at[h]
        ).start()
    small_ref[...] = small_acc[stages]

    leaving = (n_dom - 1) * peer_slots + (n_group - 1) * cross_slots
    for sweep in range(SWEEPS):
        for c in range(CHUNKS):
            whole = send.at[sweep, c, pl.ds(0, leaving)]
            pltpu.make_async_copy(whole, whole, send_sem.at[sweep, c]).wait()
    for s in range(stages):
        small_copies[s].wait_send()
        for h in range(CHUNKS):
            copies[h][s].wait_send()
    units = grad_ref.shape[1] // CHUNKS
    for h in range(CHUNKS):
        pltpu.make_async_copy(gathered.at[h], gathered.at[h], out_recv.at[h]).wait()
        rest = gathered.at[h, pl.ds(0, n_group - 1)]
        pltpu.make_async_copy(rest, rest, out_send.at[h]).wait()
        for g in range(n_group):
            grad_ref[g * share:(g + 1) * share, h * units:(h + 1) * units] = gathered[h, g]


def local(
    n_group, n_dom,
    features,
    known_mask,
    local_tile,
    peer_tile,
    cross_tile,
    peer_rows,
    cross_rows,
    labels,
    first_weight,
    first_bias,
    second_weight,
    second_bias,
):
    rows, width = features.shape
    units = first_weight.shape[1]
    classes = second_weight.shape[1]
    peer_slots, cross_slots = peer_rows.shape[3], cross_rows.shape[3]
    listed = jnp.concatenate([peer_rows.reshape(-1), cross_rows.reshape(-1)])
    halo_rows = listed.shape[0]
    pick = (listed[:, None] == jnp.arange(rows, dtype=jnp.int32)[None, :]).astype(jnp.bfloat16)
    blocks = n_group * n_dom
    stages = blocks.bit_length() - 1
    share = width // blocks
    cols = width // CHUNKS
    small_rows = -(-(classes + 2) // 8) * 8
    vmem = pl.BlockSpec(memory_space=pltpu.VMEM)
    f32, bf16 = jnp.float32, jnp.bfloat16
    dma = pltpu.SemaphoreType.DMA
    imputed, grad_first, small = pl.pallas_call(
        functools.partial(
            kernel, n_group, n_dom, peer_slots, cross_slots, rows * blocks
        ),
        out_shape=(
            jax.ShapeDtypeStruct((rows, width), f32),
            jax.ShapeDtypeStruct((width // n_dom, units), f32),
            jax.ShapeDtypeStruct((small_rows, units), f32),
        ),
        in_specs=[vmem] * 7 + [pl.BlockSpec(memory_space=pl.ANY)] + [vmem] * 3,
        out_specs=(vmem,) * 3,
        scratch_shapes=[
            pltpu.VMEM((width, units), bf16),
            pltpu.VMEM((CHUNKS, rows, cols), f32),
            pltpu.VMEM((SWEEPS, CHUNKS, halo_rows, cols), f32),
            pltpu.VMEM((SWEEPS, CHUNKS, halo_rows, cols), f32),
            pltpu.VMEM((rows, width), bf16),
            pltpu.VMEM((CHUNKS, blocks, share, units // CHUNKS), f32),
            pltpu.VMEM((CHUNKS, blocks, share, units // CHUNKS), f32),
            pltpu.VMEM((stages + 1, small_rows, units), f32),
            pltpu.VMEM((stages, small_rows, units), f32),
            pltpu.VMEM((CHUNKS, n_group, share, units // CHUNKS), f32),
            dma(()),
            dma((SWEEPS, CHUNKS)),
            dma((SWEEPS, CHUNKS)),
            dma((CHUNKS, stages)),
            dma((CHUNKS, stages)),
            dma((stages,)),
            dma((stages,)),
            dma((CHUNKS,)),
            dma((CHUNKS,)),
        ],
        compiler_params=pltpu.CompilerParams(
            collective_id=0, has_side_effects=True, vmem_limit_bytes=60 * 1024 * 1024
        ),
    )(
        features, known_mask[:, None], local_tile, peer_tile, cross_tile, pick, labels[:, None],
        first_weight, first_bias[None, :], second_weight, second_bias[None, :],
    )
    grad_second = small[:classes].T
    return (imputed, grad_first, small[classes], grad_second, small[classes + 1, :classes])


def solution(mesh):
    in_specs = (
        P(("group", "dom"), None),
        P(("group", "dom")),
        P(("group", "dom"), None),
        P(("group", "dom"), None),
        P(("group", "dom"), None),
        P("group", "dom", None, None),
        P("group", "dom", None, None),
        P(("group", "dom")),
        P(),
        P(),
        P(),
        P(),
    )
    out_specs = (P(("group", "dom"), None), P("dom", None), P(), P(), P())
    body = functools.partial(local, mesh.shape["group"], mesh.shape["dom"])
    return jax.shard_map(body, mesh=mesh, in_specs=in_specs, out_specs=out_specs, check_vma=False)
```

time: 365 us -> 138 us (0.38)
  waiting for transfers between devices: 228 us -> 0 us
  Pallas kernels: 0 us -> 122 us
  blocking collectives: 40.4 us -> 0 us
  starting transfers between devices: 31.9 us -> 0 us
  matrix products: 23 us -> 0 us
  between operations: 15.7 us -> 0.64 us
  local copies, waits for them, and re-layouts: 20.8 us -> 13.8 us
    pallas_call x0 -> x1, Pallas kernels: none -> 122 us  [local(): pl.pallas_call(functools.partial(kernel, n_group, n_dom, peer_slots, cros...]
    reduce_scatter x1 -> x0, waiting for transfers between devices: 87.1 us -> none  [local(): lax.psum_scatter(lax.dot_general(inputs, dpre, (((0,), (0,)), ((), ())),...]
    all_to_all x6 -> x0, waiting for transfers between devices: 85.6 us -> none  [the longest x3 67.8 us: fetch_halos(): lax.all_to_all(outgoing, 'dom', split_axis=0, concat_axis=0, tiled=True)]
    psum x2 -> x0, waiting for transfers between devices: 54.9 us -> none  [the longest x1 35.1 us: local(): grad_first = lax.psum(share, 'group')]
    psum x1 -> x0, blocking collectives: 40.4 us -> none  [local(): lax.psum((first_bias_term, second_term, second_bias_term), ('group', 'dom'))]
    all_to_all x6 -> x0, starting transfers between devices: 31.7 us -> none  [the longest x3 16.5 us: fetch_halos(): lax.all_to_all(leaving, 'group', split_axis=0, concat_axis=0, tiled=True)]
    dot_general x14 -> x0, matrix products: 23 us -> none  [the longest x3 6.71 us: local(): jnp.dot(peer_full, incoming, precision=highest, preferred_element_type=jn...]
    gather x6 -> x0, local copies, waits for them, and re-layouts: 10.9 us -> none  [the longest x3 6.17 us: fetch_halos(): current[peer_list.reshape(-1)]]
  transfers between devices with their start and end apart: 9 -> 0, of which waited for: 9 -> 0; matrix products, arithmetic and copies ran while one was open for 4% -> 0% of each run, Pallas kernels for 0% -> 0%
where the time goes in v1:
time: 138 us; the launch traced here: 137 us
  Pallas kernels  122 us (88%)
  local copies, waits for them, and re-layouts  13.8 us (10%)
    pallas_call x1, Pallas kernels, local(): pl.pallas_call(functools.partial(kernel, n_group, n_dom, peer_slots, cros...  122 us
    unnamed x3, local copies, waits for them, and re-layouts  5.43 us

profile of v1, /device:TPU:1, one launch (start us, length us, event | category | flops | bytes accessed | tf_op | source)
XLA Modules:
  0.0 137.5 jit_solution(3218573361468565683)
XLA Ops:
  0.6 1.4 %copy.17.keep_ref = s32[128,1]{1,0:T(8,128)} copy(s32[128,1]{0,1:T(1,128)} %bitcast.13) | data formatting | bytes 1024 | tf_op jit(solution)/shard_map/broadcast_in_dim | solution.py:315
  2.0 0.8 reshape.18
  2.8 0.8 reshape.17
  3.6 0.8 fusion.pick_ref
  4.3 1.4 %copy.18.label_ref = s32[128,1]{1,0:T(8,128)} copy(s32[128,1]{0,1:T(1,128)} %bitcast.14) | data formatting | bytes 1024 | tf_op jit(solution)/shard_map/broadcast_in_dim | solution.py:315
  5.7 1.7 %copy.19.w2_ref = bf16[1024,19]{1,0:T(8,128)(2,1)} copy(bf16[1024,19]{0,1:T(8,128)(2,1)} %param.22) | data formatting | bytes 77824 | tf_op args[10]
  7.4 122.2 %shard_map.155 = (f32[128,1024]{1,0:T(8,128)}, f32[128,1024]{1,0:T(8,128)}, f32[24,1024]{1,0:T(8,128)}) custom-call(f32[128,1024]{1,0:T(8,128)} %feat_ref.1, s32[128,1]{1,0:T(8,128)} %copy.17.keep_ref, bf16[128,128]{1,0:T(8,128)(2,1)} %local_ref.1, bf16[128,256]{1,0:T(8,128)(2,1)} %peer_ref.1, bf16[128,128]{1,0:T(8,128)(2,1)} %cross_ref.1, ...), custom_call_target="tpu_custom_call" | custom-call | tf_op jit(solution)/shard_map/pallas_call | solution.py:279
  129.6 1.4 slice.9
  131.0 1.5 %slice_bitcast_fusion = f32[1024,19]{0,1:T(8,128)} fusion(f32[24,1024]{1,0:T(8,128)} %get-tuple-element.10), kind=kLoop, calls=%fused_computation.2 | loop fusion | bytes 155648 | tf_op jit(solution)/shard_map/transpose | solution.py:318
  132.5 1.2 slice_bitcast_fusion.1
  133.7 1.9 %copy.22 = f32[128,1024]{1,0:T(8,128)} copy(f32[128,1024]{1,0:T(8,128)} %get-tuple-element.16) | data formatting | bytes 1048576
  135.6 1.9 %copy.23 = f32[128,1024]{1,0:T(8,128)} copy(f32[128,1024]{1,0:T(8,128)} %get-tuple-element.17) | data formatting | bytes 1048576
  (1 shorter events, 0.0 us)

commit v2 on v1

v2 whole, which is shorter than its diff:
```python
import functools
import math

import jax
import jax.numpy as jnp
from jax import lax
from jax.experimental import pallas as pl
from jax.experimental.pallas import tpu as pltpu
from jax.sharding import PartitionSpec as P

SWEEPS = 3
CHUNKS = 2
MESH = pl.DeviceIdType.MESH


def split(x):
    high = x.astype(jnp.bfloat16)
    low = (x - high.astype(jnp.float32)).astype(jnp.bfloat16)
    return high, low


def two_pass(a, parts):
    out = jnp.dot(a, parts[0], preferred_element_type=jnp.float32)
    return out + jnp.dot(a, parts[1], preferred_element_type=jnp.float32)


def bits_of(name, n):
    return [(name, b) for b in range(n.bit_length() - 1)]


def reduce_orders(n_group, n_dom):
    group, dom = bits_of("group", n_group), bits_of("dom", n_dom)
    bulk_a = group + dom
    bulk_b = group[:1] + dom[:1] + group[1:] + dom[1:]
    bulk_c = group[:1] + dom[1:] + group[1:] + dom[:1]
    small = dom[1:] + group[:1] + dom[:1] + group[1:]
    return [bulk_a, bulk_b, bulk_c], small


def column(row, rows):
    shape = (rows, rows)
    diagonal = lax.broadcasted_iota(jnp.int32, shape, 0) == lax.broadcasted_iota(jnp.int32, shape, 1)
    spread = jnp.broadcast_to(row.astype(jnp.float32), shape)
    return jnp.sum(jnp.where(diagonal, spread, jnp.float32(0.0)), axis=1, keepdims=True)


def kernel(
    n_group, n_dom, peer_slots, cross_slots, total_nodes,
    feat_ref, keep_ref, local_ref, peer_ref, cross_ref, peer_list, cross_list, label_ref,
    w1_hbm, b1_ref, w2_ref, b2_ref,
    imputed_ref, grad_ref, bias1_ref, second_ref, bias2_ref,
    w1_ref, cur, send, recv, inputs, lists, grads, incoming, small_acc, small_in, gathered,
    w1_sem, send_sem, recv_sem, bulk_send, bulk_recv, small_send, small_recv,
    out_send, out_recv,
):
    sizes = {"group": n_group, "dom": n_dom}
    me = {name: lax.axis_index(name) for name in sizes}
    rows, width = feat_ref.shape
    cols = width // CHUNKS
    peer_total = n_dom * peer_slots

    load_w1 = pltpu.make_async_copy(w1_hbm, w1_ref, w1_sem)
    load_w1.start()
    barrier = pltpu.get_barrier_semaphore()

    def bit(name, b):
        return lax.rem(lax.div(me[name], 1 << b), 2)

    def flipped(name, mask):
        there = me[name]
        for b in range(mask.bit_length()):
            if (mask >> b) & 1:
                there = there + (1 << b) * (1 - 2 * bit(name, b))
        return there

    for name, n in sizes.items():
        for k in range(1, n):
            pl.semaphore_signal(
                barrier, inc=1, device_id={name: flipped(name, k)}, device_id_type=MESH
            )

    local = local_ref[...]
    halo = jnp.concatenate([peer_ref[...], cross_ref[...]], axis=1)
    degree = (
        1.0
        + jnp.sum(local.astype(jnp.float32), axis=1, keepdims=True)
        + jnp.sum(halo.astype(jnp.float32), axis=1, keepdims=True)
    )
    keep = column(keep_ref[...], rows) > 0.5
    lists[...] = jnp.zeros(lists.shape, jnp.float32)
    lists[:n_dom, :peer_slots] = peer_list[...].astype(jnp.float32)
    lists[n_dom:n_dom + n_group, :cross_slots] = cross_list[...].astype(jnp.float32)
    turned = lists[...].T.astype(jnp.int32)
    pick = []
    for q in range(n_dom + n_group):
        slots = peer_slots if q < n_dom else cross_slots
        number = lax.broadcasted_iota(jnp.int32, (slots, rows), 1)
        pick.append((turned[:slots, q:q + 1] == number).astype(jnp.float32))
    pick = jnp.concatenate(pick, axis=0).astype(jnp.bfloat16)

    def exchange(sweep, c, parts):
        out = send.at[sweep, c]
        into = recv.at[sweep, c]
        send[sweep, c] = two_pass(pick, parts)
        bases = {"dom": (0, peer_slots), "group": (peer_total, cross_slots)}
        far = [("dom", k) for k in range(n_dom // 2, n_dom)]
        near = [("group", k) for k in range(n_group - 1, 0, -1)]
        near += [("dom", k) for k in range(n_dom // 2 - 1, 0, -1)]
        for name, k in far + near:
            base, slots = bases[name]
            mine = pl.ds(pl.multiple_of(base + me[name] * slots, slots), slots)
            there = flipped(name, k)
            pltpu.make_async_remote_copy(
                src_ref=out.at[pl.ds(pl.multiple_of(base + there * slots, slots), slots)],
                dst_ref=into.at[mine],
                send_sem=send_sem.at[sweep, c],
                recv_sem=recv_sem.at[sweep, c],
                device_id={name: there},
                device_id_type=MESH,
            ).start()
        for name, (base, slots) in bases.items():
            mine = pl.ds(pl.multiple_of(base + me[name] * slots, slots), slots)
            pltpu.make_async_copy(out.at[mine], into.at[mine], recv_sem.at[sweep, c]).start()

    for c in range(CHUNKS):
        now = jnp.where(keep, feat_ref[:, c * cols:(c + 1) * cols], jnp.float32(0.0))
        cur[c] = now
        if c == 0:
            pl.semaphore_wait(barrier, n_dom - 1 + n_group - 1)
        exchange(0, c, split(now))
    pre = b1_ref[...]
    for sweep in range(SWEEPS):
        if sweep + 1 == SWEEPS:
            load_w1.wait()
        for c in range(CHUNKS):
            area = slice(c * cols, (c + 1) * cols)
            now = cur[c]
            summed = now + two_pass(local, split(now))
            pltpu.make_async_copy(
                recv.at[sweep, c], recv.at[sweep, c], recv_sem.at[sweep, c]
            ).wait()
            summed = summed + two_pass(halo, split(recv[sweep, c]))
            now = jnp.where(keep, feat_ref[:, area], summed / degree)
            if sweep + 1 < SWEEPS:
                cur[c] = now
                exchange(sweep + 1, c, split(now))
            else:
                imputed_ref[:, area] = now
                inputs[area, :] = now.T.astype(jnp.bfloat16)
                pre = pre + jnp.dot(
                    now.astype(jnp.bfloat16), w1_ref[area, :], preferred_element_type=jnp.float32
                )

    sigma = jax.nn.sigmoid(pre)
    active = (pre * sigma).astype(jnp.bfloat16)
    w2 = w2_ref[...]
    logits = b2_ref[...] + lax.dot_general(
        active, w2, (((1,), (1,)), ((), ())), preferred_element_type=jnp.float32
    )
    shifted = logits - jnp.max(logits, axis=1, keepdims=True)
    expo = jnp.exp(shifted)
    probs = expo / jnp.sum(expo, axis=1, keepdims=True)
    classes = w2.shape[0]
    label = column(label_ref[...], rows).astype(jnp.int32)
    hot = label == lax.broadcasted_iota(jnp.int32, (rows, classes), 1)
    dlogits = (probs - hot.astype(jnp.float32)) / jnp.float32(math.sqrt(total_nodes))
    dlogits_b = dlogits.astype(jnp.bfloat16)
    back = jnp.dot(dlogits_b, w2, preferred_element_type=jnp.float32)
    dpre32 = back * sigma * (1.0 + pre * (1.0 - sigma))
    dpre = dpre32.astype(jnp.bfloat16)

    orders, small_order = reduce_orders(n_group, n_dom)
    stages = len(small_order)

    def partner(name, b):
        return {name: flipped(name, 1 << b)}

    small_acc[0] = jnp.zeros(small_acc.shape[1:], jnp.float32)
    small_acc[0, :classes] = lax.dot_general(
        dlogits_b, active, (((0,), (0,)), ((), ())), preferred_element_type=jnp.float32
    )
    small_acc[0, classes:classes + 1] = jnp.sum(dpre.astype(jnp.float32), axis=0, keepdims=True)
    small_acc[0, classes + 1:classes + 2, :classes] = jnp.sum(dlogits, axis=0, keepdims=True)

    def small_copy(s):
        return pltpu.make_async_remote_copy(
            src_ref=small_acc.at[s],
            dst_ref=small_in.at[s],
            send_sem=small_send.at[s],
            recv_sem=small_recv.at[s],
            device_id=partner(*small_order[s]),
            device_id_type=MESH,
        )

    deep, share = width // n_dom, width // n_dom // n_group
    blocks = n_group * n_dom

    def place(order, where):
        at = 0
        for name, b in order:
            at = 2 * at + ((where[name] >> b) & 1)
        return at

    parts, lanes = grads.shape[0], grads.shape[3]
    orders = [orders[h % len(orders)] for h in range(parts)]
    start = [0] * parts
    copies = [[] for _ in range(parts)]

    def bulk_start(s, h):
        half = blocks >> (s + 1)
        name, b = orders[h][s]
        mine = bit(name, b)
        copy = pltpu.make_async_remote_copy(
            src_ref=grads.at[h, pl.ds(start[h] + (1 - mine) * half, half)],
            dst_ref=incoming.at[h, pl.ds(blocks - 2 * half, half)],
            send_sem=bulk_send.at[h, s],
            recv_sem=bulk_recv.at[h, s],
            device_id=partner(name, b),
            device_id_type=MESH,
        )
        copy.start()
        copies[h].append(copy)
        start[h] = start[h] + mine * half

    small_copies = [small_copy(0)]
    small_copies[0].start()
    together = max(1, 256 // lanes)
    for first in range(0, parts, together):
        group_of = range(first, first + together)
        term = jnp.dot(
            inputs[...], dpre[:, first * lanes:(first + together) * lanes],
            preferred_element_type=jnp.float32,
        )
        for h in group_of:
            for d in range(n_dom):
                for g in range(n_group):
                    top = (d * n_group + g) * share
                    grads[h, place(orders[h], {"group": g, "dom": d})] = term[
                        top:top + share, (h - first) * lanes:(h - first + 1) * lanes
                    ]
            bulk_start(0, h)

    group_bits = bits_of("group", n_group)
    my_place = 0
    for name, b in group_bits:
        my_place = 2 * my_place + bit(name, b)
    rounds = [[] for _ in range(parts)]

    def share_out(r, h):
        name, b = group_bits[len(group_bits) - 1 - r]
        held = pl.ds(lax.div(my_place, 1 << r) * (1 << r), 1 << r)
        copy = pltpu.make_async_remote_copy(
            src_ref=gathered.at[h, held],
            dst_ref=gathered.at[h, held],
            send_sem=out_send.at[h, r],
            recv_sem=out_recv.at[h, r],
            device_id=partner(name, b),
            device_id_type=MESH,
        )
        copy.start()
        rounds[h].append(copy)

    for s in range(stages):
        half = blocks >> (s + 1)
        for h in range(parts):
            copies[h][s].wait_recv()
            kept = pl.ds(start[h], half)
            total = grads[h, kept] + incoming[h, pl.ds(blocks - 2 * half, half)]
            if s + 1 < stages:
                grads[h, kept] = total
                bulk_start(s + 1, h)
            else:
                gathered[h, pl.ds(my_place, 1)] = total
                share_out(0, h)
        small_copies[s].wait_recv()
        small_acc[s + 1] = small_acc[s] + small_in[s]
        if s + 1 < stages:
            small_copies.append(small_copy(s + 1))
            small_copies[-1].start()
    second_ref[...] = small_acc[stages, :classes]
    bias1_ref[...] = small_acc[stages, classes:classes + 1]
    bias2_ref[...] = small_acc[stages, classes + 1:classes + 2, :classes]
    for r in range(len(group_bits)):
        for h in range(parts):
            rounds[h][r].wait_recv()
            if r + 1 < len(group_bits):
                share_out(r + 1, h)
    for h in range(parts):
        for g in range(n_group):
            grad_ref[g * share:(g + 1) * share, h * lanes:(h + 1) * lanes] = gathered[
                h, place(group_bits, {"group": g})
            ]

    leaving = (n_dom - 1) * peer_slots + (n_group - 1) * cross_slots
    for sweep in range(SWEEPS):
        for c in range(CHUNKS):
            whole = send.at[sweep, c, pl.ds(0, leaving)]
            pltpu.make_async_copy(whole, whole, send_sem.at[sweep, c]).wait()
    for s in range(stages):
        small_copies[s].wait_send()
        for h in range(parts):
            copies[h][s].wait_send()
    for h in range(parts):
        for copy in rounds[h]:
            copy.wait_send()


def finish(count, *refs):
    sems = refs[-1]
    copies = [
        pltpu.make_async_copy(refs[i], refs[count + i], sems.at[i]) for i in range(count)
    ]
    for copy in copies:
        copy.start()
    for copy in copies:
        copy.wait()


def local(
    n_group, n_dom,
    features,
    known_mask,
    local_tile,
    peer_tile,
    cross_tile,
    peer_rows,
    cross_rows,
    labels,
    first_weight,
    first_bias,
    second_weight,
    second_bias,
):
    rows, width = features.shape
    units = first_weight.shape[1]
    classes = second_weight.shape[1]
    peer_slots, cross_slots = peer_rows.shape[3], cross_rows.shape[3]
    halo_rows = n_dom * peer_slots + n_group * cross_slots
    blocks = n_group * n_dom
    stages = blocks.bit_length() - 1
    share = width // blocks
    cols = width // CHUNKS
    small_rows = -(-(classes + 2) // 8) * 8
    vmem = pl.BlockSpec(memory_space=pltpu.VMEM)
    f32, bf16 = jnp.float32, jnp.bfloat16
    dma = pltpu.SemaphoreType.DMA
    parts = 8 if share % 8 == 0 else 2
    list_shape = (-(-(n_dom + n_group) // 128) * 128, -(-max(peer_slots, cross_slots) // 128) * 128)
    bulk = pltpu.VMEM((parts, blocks, share, units // parts), f32)
    rounds = n_group.bit_length() - 1
    shapes = (
        jax.ShapeDtypeStruct((rows, width), f32),
        jax.ShapeDtypeStruct((width // n_dom, units), f32),
        jax.ShapeDtypeStruct((1, units), f32),
        jax.ShapeDtypeStruct((classes, units), f32),
        jax.ShapeDtypeStruct((1, classes), f32),
    )
    results = pl.pallas_call(
        functools.partial(
            kernel, n_group, n_dom, peer_slots, cross_slots, rows * blocks
        ),
        out_shape=shapes,
        in_specs=[vmem] * 8 + [pl.BlockSpec(memory_space=pl.ANY)] + [vmem] * 3,
        out_specs=(vmem,) * 5,
        scratch_shapes=[
            pltpu.VMEM((width, units), bf16),
            pltpu.VMEM((CHUNKS, rows, cols), f32),
            pltpu.VMEM((SWEEPS, CHUNKS, halo_rows, cols), f32),
            pltpu.VMEM((SWEEPS, CHUNKS, halo_rows, cols), f32),
            pltpu.VMEM((width, rows), bf16),
            pltpu.VMEM(list_shape, f32),
            bulk,
            bulk,
            pltpu.VMEM((stages + 1, small_rows, units), f32),
            pltpu.VMEM((stages, small_rows, units), f32),
            pltpu.VMEM((parts, n_group, share, units // parts), f32),
            dma(()),
            dma((SWEEPS, CHUNKS)),
            dma((SWEEPS, CHUNKS)),
            dma((parts, stages)),
            dma((parts, stages)),
            dma((stages,)),
            dma((stages,)),
            dma((parts, rounds)),
            dma((parts, rounds)),
        ],
        compiler_params=pltpu.CompilerParams(
            collective_id=0, has_side_effects=True, vmem_limit_bytes=60 * 1024 * 1024
        ),
    )(
        features, known_mask[None, :], local_tile, peer_tile, cross_tile,
        peer_rows.reshape(n_dom, peer_slots), cross_rows.reshape(n_group, cross_slots),
        labels[None, :], first_weight, first_bias[None, :], second_weight.T, second_bias[None, :],
    )
    imputed, grad_first, bias1, second, bias2 = pl.pallas_call(
        functools.partial(finish, len(shapes)),
        out_shape=shapes,
        in_specs=[pl.BlockSpec(memory_space=pl.ANY)] * len(shapes),
        out_specs=(vmem,) * len(shapes),
        scratch_shapes=[dma((len(shapes),))],
    )(*results)
    return (imputed, grad_first, bias1[0], second.T, bias2[0])


def solution(mesh):
    in_specs = (
        P(("group", "dom"), None),
        P(("group", "dom")),
        P(("group", "dom"), None),
        P(("group", "dom"), None),
        P(("group", "dom"), None),
        P("group", "dom", None, None),
        P("group", "dom", None, None),
        P(("group", "dom")),
        P(),
        P(),
        P(),
        P(),
    )
    out_specs = (P(("group", "dom"), None), P("dom", None), P(), P(), P())
    body = functools.partial(local, mesh.shape["group"], mesh.shape["dom"])
    return jax.shard_map(body, mesh=mesh, in_specs=in_specs, out_specs=out_specs, check_vma=False)
```

time: 138 us -> 112 us (0.81)
  local copies, waits for them, and re-layouts: 13.8 us -> 0 us
  Pallas kernels: 122 us -> 111 us
    pallas_call x1, Pallas kernels: 122 us -> 109 us  [local(): pl.pallas_call(functools.partial(kernel, n_group, n_dom, peer_slots, cros...]
    unnamed x3 -> x0, local copies, waits for them, and re-layouts: 5.43 us -> none
    broadcast_in_dim x2 -> x0, local copies, waits for them, and re-layouts: 2.77 us -> none  [the longest x1 1.39 us: local(): known_mask[:, None]]
    pallas_call x0 -> x1, Pallas kernels: none -> 2.26 us  [local(): pl.pallas_call(functools.partial(finish, len(shapes)), out_shape=shapes,...]
    transpose x1 -> x0, local copies, waits for them, and re-layouts: 1.54 us -> none  [local(): grad_second = small[:classes].T]
    reshape x2 -> x0, local copies, waits for them, and re-layouts: 1.53 us -> none  [local(): listed = jnp.concatenate([peer_rows.reshape(-1), cross_rows.reshape(-1)])]
where the time goes in v2:
time: 112 us
  Pallas kernels  111 us (99%)
    pallas_call x1, Pallas kernels, local(): pl.pallas_call(functools.partial(kernel, n_group, n_dom, peer_slots, cros...  109 us
    pallas_call x1, Pallas kernels, local(): pl.pallas_call(functools.partial(finish, len(shapes)), out_shape=shapes,...  2.26 us

profile of v2, /device:TPU:1, one launch (start us, length us, event | category | flops | bytes accessed | tf_op | source)
XLA Modules:
  0.0 111.6 jit_solution(6803519625049845251)
XLA Ops:
  0.6 108.6 %shard_map.155 = (f32[128,1024]{1,0:T(8,128)}, f32[128,1024]{1,0:T(8,128)}, f32[1,1024]{1,0:T(1,128)}, f32[19,1024]{1,0:T(8,128)}, f32[1,19]{1,0:T(1,128)}) custom-call(f32[128,1024]{1,0:T(8,128)} %feat_ref.1, s32[1,128]{1,0:T(1,128)} %bitcast.14, bf16[128,128]{1,0:T(8,128)(2,1)} %local_ref.1, bf16[128,256]{1,0:T(8,128)(2,1)} %peer_ref.1, ...), custom_call_target="tpu_custom_call" | custom-call | tf_op jit(solution)/shard_map/pallas_call | solution.py:358
  109.3 2.3 %shard_map.156 = (f32[128,1024]{1,0:T(8,128)}, f32[128,1024]{1,0:T(8,128)}, f32[1,1024]{1,0:T(1,128)}, f32[19,1024]{1,0:T(8,128)}, f32[1,19]{1,0:T(1,128)}) custom-call(f32[128,1024]{1,0:T(8,128)} %get-tuple-element.15.refs_0_, f32[128,1024]{1,0:T(8,128)} %get-tuple-element.16.refs_1_, f32[1,1024]{1,0:T(1,128)} %get-tuple-element.17.refs_2_, ...), custom_call_target="tpu_custom_call" | custom-call | tf_op jit(solution)/shard_map/pallas_call | solution.py:395
